TPU v7x, 32 devices: a whole 2x2x4 slice. The times are simulated.
32 devices in a mesh: chan: 2 (over x), bl: 16 (over z, y, core).
Axes of the slice: x: 2, y: 2, z: 4, core: 2. Of those that a mesh axis runs over, the one named last changes fastest.
Arguments:
- vis: bfloat16 [2, 8, 8192, 256], P(None, 'chan', 'bl'), may hold values from -6 to 6
- station_pair_index: int32 [8192, 2], P('bl'), may hold values from 0 to 511
- station_coords: float32 [512, 2], replicated, may hold values from -1 to 1
- dir_lm: float32 [60, 2], replicated, may hold values from -0.5 to 0.5
- time_beam: float32 [60, 256], replicated, may hold values from -6 to 6
- dir_cluster: int32 [60], replicated, may hold values from 0 to 11, as said below
- seed_block: int32 [64, 256, 8], P('bl'), may hold values from -8 to 8
Outputs:
- clean: bfloat16 [2, 8, 8192, 256], P(None, 'chan', 'bl')
- gains: float32 [64, 12], P('bl')
- consensus: float32 [12], replicated
Inputs may be any that keep to these rules, and one draw needn't show every extreme that they name: `dir_cluster`: every cluster is named by some direction.
All inputs are finite; a program needn't handle non-finite values.
Results may differ from a plain program's by a relative error of at most 0.0029.
The roundings to bfloat16 on the way count: a program that leaves them out, or rounds other values in their place, can miss the bound.
Values sent between devices are 32-bit elements; how exact they have to be, the bound alone decides.
A program may use at most 64 MiB of HBM per device.

v0:
```python
import jax
import jax.numpy as jnp
from jax import lax
from jax.sharding import PartitionSpec as P

CL = 12
SUB_ITERS = 3
ADMM_ITERS = 6


HIGHEST = lax.Precision.HIGHEST
PHASE_SCALE = 20.0
RHO_SCALE = 0.5


def orthonormal(block):
    square = jnp.einsum("jtk,jtl->jkl", block, block, precision=HIGHEST)
    lower = jnp.linalg.cholesky(square)
    solved = jax.scipy.linalg.solve_triangular(lower, jnp.swapaxes(block, 1, 2), lower=True)
    return jnp.swapaxes(solved, 1, 2)


def beam_fit(beam_proj, basis_wide, time_beam):
    coeffs = jnp.einsum("jdt,jtk->jdk", beam_proj, basis_wide, precision=HIGHEST)
    inner = beam_proj - jnp.einsum("jdk,jtk->jdt", coeffs, basis_wide, precision=HIGHEST)
    return jnp.sum(inner * time_beam[None], axis=-1)


def consensus_total(values):
    return lax.psum(values, "bl")


def per_device(vis, station_pair_index, station_coords, dir_lm, time_beam, dir_cluster, seed_block):
    chan_dev = vis.shape[1]
    base_dev = vis.shape[2]
    times = vis.shape[3]
    tiles_dev = seed_block.shape[0]
    tile = base_dev // tiles_dev
    dirs = dir_lm.shape[0]
    channels = chan_dev * lax.axis_size("chan")
    tiles_all = tiles_dev * lax.axis_size("bl")
    stations = jnp.arange(station_coords.shape[0])[None, :]
    picker = (station_pair_index[:, 0:1] == stations).astype(jnp.float32) - (
        station_pair_index[:, 1:2] == stations
    ).astype(jnp.float32)
    uv = jnp.dot(picker, station_coords, precision=HIGHEST)
    geo = jnp.dot(dir_lm, uv.T, precision=HIGHEST)
    chan = (lax.axis_index("chan") * chan_dev + jnp.arange(chan_dev)).astype(jnp.float32)
    freq = 1.0 + chan / channels
    phase = (PHASE_SCALE * freq)[None, :, None] * geo[:, None, :]
    response = jnp.stack([jnp.cos(phase), jnp.sin(phase)], axis=1).astype(jnp.bfloat16)
    resp_tiles = response.reshape(dirs, 2, chan_dev, tiles_dev, tile)
    vis_tiles = vis.reshape(2, chan_dev, tiles_dev, tile, times)
    beam_part = jnp.einsum(
        "dpcjb,pcjbt->jdt", resp_tiles, vis_tiles, preferred_element_type=jnp.float32
    )
    model_part = jnp.einsum(
        "dpcjb,epcjb->jde", resp_tiles, resp_tiles, preferred_element_type=jnp.float32
    )
    block = seed_block.astype(jnp.float32)
    gram_part = jnp.einsum(
        "pcjbt,pcjbs->jts", vis_tiles, vis_tiles, preferred_element_type=jnp.float32
    )
    gram = lax.psum(gram_part, "chan")
    for step in range(SUB_ITERS):
        block = orthonormal(jnp.einsum("jts,jsk->jtk", gram, block, precision=HIGHEST))
    basis = block.astype(jnp.bfloat16)
    basis_wide = basis.astype(jnp.float32)
    proj = jnp.einsum("pcjbt,jtk->pcjbk", vis_tiles, basis, preferred_element_type=jnp.float32)
    correction = jnp.einsum("pcjbk,jtk->pcjbt", proj, basis_wide, precision=HIGHEST)
    clean = (
        (vis_tiles.astype(jnp.float32) - correction)
        .astype(jnp.bfloat16)
        .reshape(2, chan_dev, base_dev, times)
    )
    rhs_part = beam_fit(beam_part, basis_wide, time_beam)
    rhs_dir, model_gram = lax.psum((rhs_part, model_part), "chan")
    beam_gram = jnp.dot(time_beam, time_beam.T, precision=HIGHEST)
    member = (dir_cluster[:, None] == jnp.arange(CL)[None, :]).astype(jnp.float32)
    weighted = model_gram * beam_gram[None]
    normal_matrix = jnp.einsum("dk,jde->jke", member, weighted, precision=HIGHEST)
    normal_matrix = jnp.einsum("jke,el->jkl", normal_matrix, member, precision=HIGHEST)
    rhs = jnp.einsum("dk,jd->jk", member, rhs_dir, precision=HIGHEST)
    rho = RHO_SCALE * jnp.trace(normal_matrix, axis1=1, axis2=2) / CL
    system = normal_matrix + rho[:, None, None] * jnp.eye(CL, dtype=jnp.float32)[None]
    lower = jnp.linalg.cholesky(system)
    center = jnp.zeros((CL,), jnp.float32)
    dual = jnp.zeros((tiles_dev, CL), jnp.float32)
    solved = jnp.zeros((tiles_dev, CL), jnp.float32)
    for step in range(ADMM_ITERS):
        target = rhs + rho[:, None] * (center[None, :] - dual)
        solved = jax.scipy.linalg.cho_solve((lower, True), target[..., None])[..., 0]
        center = consensus_total(jnp.sum(solved + dual, axis=0)) / tiles_all
        dual = dual + solved - center[None, :]
    factor = jnp.sqrt(jnp.float32(channels * tile * times))
    return (clean, solved * factor, center * factor)


def solution(mesh):
    placed = (P(None, "chan", "bl", None), P("bl", None), P(), P(), P(), P(), P("bl", None, None))
    return jax.shard_map(
        per_device,
        mesh=mesh,
        in_specs=placed,
        out_specs=(P(None, "chan", "bl", None), P("bl", None), P()),
        check_vma=False,
    )
```

profile of v0, /device:TPU:0, one launch (start us, length us, event | category | flops | bytes accessed | tf_op | source)
XLA Modules:
  0.0 301.5 jit_solution(3390902510495110768)
XLA Ops:
  7.2 4.1 %fusion.7 = f32[4,256,256]{2,1,0:T(8,128)} fusion(bf16[2,4,4,128,256]{4,3,2,1,0:T(8,128)(2,1)} %bitcast.243), kind=kOutput, calls=%fused_computation.8 | convolution fusion | flops 536870912 | bytes 3145728 | tf_op jit(solution)/shard_map/pcjbt,pcjbs->jts/dot_general | solution.py:61
  11.4 1.2 fusion.18
  12.7 0.3 convolution_bitcast_fusion.1
  13.1 2.0 fusion.22
  15.1 0.9 convolution_bitcast_fusion
  16.1 0.6 iota_compare_fusion.10
  16.6 0.6 iota_compare_fusion.9
  17.2 0.6 iota_compare_fusion.4
  17.8 0.6 fusion.68
  18.4 0.8 fusion.85
  19.2 0.5 fusion.10
  19.7 34.6 %all-reduce.3.cloned.1.call-done = f32[4,256,256]{2,1,0:T(8,128)} async-done(((f32[4,256,256]{2,1,0:T(8,128)}), f32[4,256,256]{2,1,0:T(8,128)}) %all-reduce.3.cloned.1.call-update) | async-done | bytes 1048592 | tf_op jit(solution)/shard_map/psum | solution.py:64
  54.3 2.3 fusion.53
  56.6 0.2 fusion.80
  56.9 0.6 fusion.62
  57.5 3.6 %custom-call.25 = f32[4,8,8]{2,1,0:T(8,128)S(1)} custom-call(f32[4,8,8]{2,1,0:T(8,128)} %fusion.62), custom_call_target="Cholesky" | custom-call | tf_op jit(solution)/shard_map/jit(cholesky)/cholesky | solution.py:18
  61.0 0.7 select_reduce_fusion.4
  61.9 0.8 select_bitcast_fusion.3
  62.7 2.5 custom-call.26
  65.2 0.2 fusion.51
  65.4 2.2 fusion.81
  67.6 0.2 fusion.82
  67.9 0.6 fusion.60
  68.5 3.6 %custom-call.27 = f32[4,8,8]{2,1,0:T(8,128)S(1)} custom-call(f32[4,8,8]{2,1,0:T(8,128)} %fusion.60), custom_call_target="Cholesky" | custom-call | tf_op jit(solution)/shard_map/jit(cholesky)/cholesky | solution.py:18
  72.1 0.7 select_reduce_fusion.3
  72.9 1.4 select_bitcast_fusion.2
  74.3 3.3 %custom-call.28 = f32[4,1,8,8]{2,3,1,0:T(8,128)S(1)} custom-call(f32[4,1,8,8]{3,2,1,0:T(8,128)} %select_bitcast_fusion.2), custom_call_target="InvertDiagBlocksLowerTriangular" | custom-call | tf_op jit(solution)/shard_map/jit(_solve_triangular)/vmap()/triangular_solve | solution.py:19
  77.5 0.2 fusion.49
  77.8 1.0 fusion.83
  78.8 0.2 fusion.84
  79.0 2.9 custom-call.29
  81.9 0.7 select_reduce_fusion.2
  82.8 0.8 select_bitcast_fusion.1
  83.5 2.5 custom-call.30
  86.0 0.2 convolution_convert_fusion
  86.3 0.2 fusion.86
  86.5 0.4 fusion.14
  87.0 9.2 %all-reduce = (f32[4,60]{1,0:T(4,128)S(1)}, f32[4,60,60]{2,1,0:T(8,128)S(1)}) all-reduce(f32[4,60]{1,0:T(4,128)S(1)} %fusion.14, f32[4,60,60]{2,1,0:T(8,128)} %convolution_bitcast_fusion), channel_id=1, replica_groups=mesh['chan'=2,'bl'=16] {'chan'}, use_global_device_ids=true, to_apply=%region_8.11 | all-reduce | flops 14640 | bytes 117120 | tf_op jit(solution)/shard_map/psum | solution.py:77
  96.2 0.9 convolution_bitcast_fusion.2
  97.1 0.9 select_reduce_fusion.1
  98.3 4.4 %custom-call.15 = f32[4,12,12]{2,1,0:T(8,128)S(1)} custom-call(f32[4,12,12]{2,1,0:T(8,128)S(1)} %fusion.47), custom_call_target="Cholesky" | custom-call | tf_op jit(solution)/shard_map/jit(cholesky)/cholesky | solution.py:86
  102.8 0.8 select_bitcast_fusion
  103.6 3.7 %custom-call.36 = f32[4,1,12,12]{2,3,1,0:T(8,128)S(1)} custom-call(f32[4,1,12,12]{3,2,1,0:T(8,128)S(1)} %select_bitcast_fusion), custom_call_target="InvertDiagBlocksLowerTriangular" | custom-call | tf_op jit(solution)/shard_map/jit(_cho_solve)/vmap()/triangular_solve | solution.py:92
  107.3 0.8 broadcast_add_fusion
  108.0 0.2 convolution_bitcast_fusion.8
  108.3 0.2 fusion.28
  108.5 0.6 fusion.15
  109.1 31.4 %psum.66 = f32[12]{0:T(128)S(1)} all-reduce(f32[12]{0:T(128)S(1)} %reduce_sum.75), channel_id=1, replica_groups=mesh['chan'=2,'bl'=16] {'bl'}, use_global_device_ids=true, to_apply=%region_10.14 | all-reduce | flops 12 | bytes 96 | tf_op jit(solution)/shard_map/psum | solution.py:30
  140.7 0.2 fusion.31
  140.9 29.5 %psum.67 = f32[12]{0:T(128)S(1)} all-reduce(f32[12]{0:T(128)S(1)} %get-tuple-element.14), channel_id=1, replica_groups=mesh['chan'=2,'bl'=16] {'bl'}, use_global_device_ids=true, to_apply=%region_12.16 | all-reduce | flops 12 | bytes 96 | tf_op jit(solution)/shard_map/psum | solution.py:30
  170.5 0.2 convolution_bitcast_fusion.6
  170.7 0.2 fusion.34
  170.9 29.5 %psum.68 = f32[12]{0:T(128)S(1)} all-reduce(f32[12]{0:T(128)S(1)} %get-tuple-element.12), channel_id=1, replica_groups=mesh['chan'=2,'bl'=16] {'bl'}, use_global_device_ids=true, to_apply=%region_14.18 | all-reduce | flops 12 | bytes 96 | tf_op jit(solution)/shard_map/psum | solution.py:30
  200.4 0.2 convolution_bitcast_fusion.5
  200.6 0.2 fusion.37
  200.8 29.5 %psum.69 = f32[12]{0:T(128)S(1)} all-reduce(f32[12]{0:T(128)S(1)} %get-tuple-element.10), channel_id=1, replica_groups=mesh['chan'=2,'bl'=16] {'bl'}, use_global_device_ids=true, to_apply=%region_16.20 | all-reduce | flops 12 | bytes 96 | tf_op jit(solution)/shard_map/psum | solution.py:30
  230.5 0.2 fusion.40
  230.7 29.5 %psum.70 = f32[12]{0:T(128)S(1)} all-reduce(f32[12]{0:T(128)S(1)} %get-tuple-element.8), channel_id=1, replica_groups=mesh['chan'=2,'bl'=16] {'bl'}, use_global_device_ids=true, to_apply=%region_18.22 | all-reduce | flops 12 | bytes 96 | tf_op jit(solution)/shard_map/psum | solution.py:30
  260.5 0.2 fusion.43
  260.7 0.6 add_reduce_fusion
  261.3 29.5 %psum.71 = f32[12]{0:T(128)S(1)} all-reduce(f32[12]{0:T(128)S(1)} %get-tuple-element.20), channel_id=1, replica_groups=mesh['chan'=2,'bl'=16] {'bl'}, use_global_device_ids=true, to_apply=%region_20.24 | all-reduce | flops 12 | bytes 96 | tf_op jit(solution)/shard_map/psum | solution.py:30
  290.7 0.5 broadcast_multiply_fusion.1
  291.2 2.0 fusion
  293.2 1.5 copy.50
  (51 shorter events, 2.1 us)
Async XLA Ops:
  7.2 4.2 %copy-start = (f32[512,2]{0,1:T(2,128)S(1)}, f32[512,2]{0,1:T(2,128)}, u32[]{:S(2)}) copy-start(f32[512,2]{0,1:T(2,128)} %param.14) | copy-start | bytes 12292
  7.2 47.1 %all-reduce.3.cloned.1.call-start = ((), (), s32[]{:S(2)}) async-start(), calls=%async_computation | async-start | bytes 2097152 | tf_op jit(solution)/shard_map/psum | solution.py:64
  7.2 4.2 %copy-start.5 = (s32[512,2]{0,1:T(2,128)S(1)}, s32[512,2]{0,1:T(2,128)}, u32[]{:S(2)}) copy-start(s32[512,2]{0,1:T(2,128)} %param.13) | copy-start | bytes 12292
  7.2 5.4 %copy-start.6 = (f32[60,2]{0,1:T(2,128)S(1)}, f32[60,2]{0,1:T(2,128)}, u32[]{:S(2)}) copy-start(f32[60,2]{0,1:T(2,128)} %param.15) | copy-start | bytes 1444
  11.3 7.1 %copy-start.3 = (f32[60,256]{1,0:T(8,128)S(1)}, f32[60,256]{1,0:T(8,128)}, u32[]{:S(2)}) copy-start(f32[60,256]{1,0:T(8,128)} %param.16) | copy-start | bytes 184324
  11.3 7.9 %copy-start.2 = (bf16[2,4,512,256]{3,2,1,0:T(8,128)(2,1)S(1)}, bf16[2,4,512,256]{3,2,1,0:T(8,128)(2,1)}, u32[]{:S(2)}) copy-start(bf16[2,4,512,256]{3,2,1,0:T(8,128)(2,1)} %param.12) | copy-start | bytes 6291460
  54.3 23.5 %copy-start.1 = (f32[4,256,256]{2,1,0:T(8,128)S(1)}, f32[4,256,256]{2,1,0:T(8,128)}, u32[]{:S(2)}) copy-start(f32[4,256,256]{2,1,0:T(8,128)} %all-reduce.3.cloned.1.call-done) | copy-start | bytes 3145732
  68.5 29.7 %copy-start.4 = (f32[12,12]{1,0:T(8,128)S(1)}, f32[12,12]{1,0:T(8,128)}, u32[]{:S(2)}) copy-start(f32[12,12]{1,0:T(8,128)} %get-tuple-element.29) | copy-start | bytes 1732
Sparse Core Ops, SparseCore 0:
  11.5 42.7 all-reduce.2
where the time goes:
time: 302 us
  blocking collectives  188 us (62%)
  other arithmetic  40.2 us (13%)
  waiting for transfers between devices  34.6 us (11%)
  matrix products  22.6 us (7%)
  between operations  14.2 us (5%)
    psum x6, blocking collectives, consensus_total(): return lax.psum(values, 'bl')  179 us
    psum x1, waiting for transfers between devices, per_device(): gram = lax.psum(gram_part, 'chan')  34.6 us
    another operation x10, other arithmetic, orthonormal(): lower = jnp.linalg.cholesky(square)  13.2 us
    another operation x7, other arithmetic, orthonormal(): jax.scipy.linalg.solve_triangular(lower, jnp.swapaxes(block, 1, 2), lower...  11.7 us
    psum x1, blocking collectives, per_device(): rhs_dir, model_gram = lax.psum((rhs_part, model_part), 'chan')  9.23 us
  transfers between devices with their start and end apart: 1, of which 1 were waited for; matrix products, arithmetic and copies ran while one was open for 3% of the time, Pallas kernels for 0%

commit v1 on v0

v1 whole, which is shorter than its diff:
```python
import functools

import jax
import jax.numpy as jnp
from jax import lax
from jax.experimental import pallas as pl
from jax.experimental.pallas import tpu as pltpu
from jax.sharding import PartitionSpec as P

CL = 12
SUB_ITERS = 3
ADMM_ITERS = 6
PHASE_SCALE = 20.0
RHO_SCALE = 0.5

HIGHEST = lax.Precision.HIGHEST
MESH = pl.DeviceIdType.MESH
F32 = jnp.float32
BF16 = jnp.bfloat16
LANES = 128
GROUP = 16
NT = (((1,), (1,)), ((), ()))
TN = (((0,), (0,)), ((), ()))


def split3(x):
    a = x.astype(BF16).astype(F32)
    rest = x - a
    b = rest.astype(BF16).astype(F32)
    return a, b, rest - b


def sincos(phase):
    k = jnp.floor(phase * F32(0.6366197723675814) + F32(0.5))
    r = phase - k * F32(1.5703125)
    r = r - k * F32(4.837512969970703125e-4)
    r = r - k * F32(7.54978995489188216e-8)
    r2 = r * r
    s = r + r * r2 * (F32(-1.6666654611e-1) + r2 * (F32(8.3321608736e-3) + r2 * F32(-1.9515295891e-4)))
    c = (F32(1.0) - F32(0.5) * r2) + r2 * r2 * (
        F32(4.166664568298827e-2) + r2 * (F32(-1.388731625493765e-3) + r2 * F32(2.443315711809948e-5))
    )
    ki = k.astype(jnp.int32)
    odd = (ki & 1) == 1
    cos = jnp.where(odd, s, c)
    sin = jnp.where(odd, c, s)
    cos = jnp.where(((ki + 1) & 2) == 2, -cos, cos)
    sin = jnp.where((ki & 2) == 2, -sin, sin)
    return cos, sin


def orthonormal(rows):
    sub = lax.broadcasted_iota(jnp.int32, (1, rows.shape[1], 1), 1)
    for k in range(rows.shape[1]):
        lead = rows[:, k : k + 1, :]
        dots = jnp.sum(rows * lead, axis=-1, keepdims=True)
        if k + 1 < rows.shape[1]:
            coef = jnp.where(sub > k, dots / dots[:, k : k + 1, :], F32(0.0))
            rows = rows - coef * lead
    norm = jnp.sum(rows * rows, axis=-1, keepdims=True)
    return rows / jnp.sqrt(norm)


def main_kernel(
    n_chan, n_bl, channels,
    vis_ref, pair_ref, coords_ref, lm_ref, tb_ref, cluster_ref, seed_ref,
    basis_ref, gains_ref, cons_ref,
    gsplit, resp, lmp, tbp, clp, coord_rows, uv_ref, beam, bsplit,
    ybuf, nbuf, mbuf, vbuf, send_sems, recv_sems,
):
    chan_dev, base_dev, times = vis_ref.shape[1:]
    tiles, rank = seed_ref.shape[0], seed_ref.shape[1]
    tile = base_dev // tiles
    dirs = lm_ref.shape[0]
    dpad = lmp.shape[0]
    stations = coords_ref.shape[1]
    n_all = n_chan * n_bl
    tiles_all = tiles * n_bl
    my_chan = lax.axis_index("chan")
    my_bl = lax.axis_index("bl")
    my_id = my_chan * n_bl + my_bl

    def everyone(off):
        other = lax.rem(my_id + off, n_all)
        return (lax.div(other, n_bl), lax.rem(other, n_bl))

    def along_chan(off):
        return (lax.rem(my_chan + off, n_chan), my_bl)

    def along_bl(off):
        return (my_chan, lax.rem(my_bl + off, n_bl))

    barrier = pltpu.get_barrier_semaphore()

    @pl.loop(1, n_all)
    def _(off):
        pl.semaphore_signal(barrier, inc=1, device_id=everyone(off), device_id_type=MESH)

    def push(buf, me, n, peer, phase):
        @pl.loop(1, n)
        def _(off):
            pltpu.make_async_remote_copy(
                src_ref=buf.at[me],
                dst_ref=buf.at[me],
                send_sem=send_sems.at[phase],
                recv_sem=recv_sems.at[phase],
                device_id=peer(off),
                device_id_type=MESH,
            ).start()

    def arrived(buf, n, phase):
        part = buf.at[pl.ds(0, n - 1)]
        pltpu.make_async_copy(part, part, recv_sems.at[phase]).wait()

    def sent(buf, n, phase):
        part = buf.at[pl.ds(0, n - 1)]
        pltpu.make_async_copy(part, part, send_sems.at[phase]).wait()

    def total(buf, n):
        out = buf[0]
        for i in range(1, n):
            out = out + buf[i]
        return out

    def vis_tile(j):
        return vis_ref[:, :, j * tile : (j + 1) * tile, :].reshape(2 * chan_dev * tile, times)

    first = []
    for j in range(tiles):
        v = vis_tile(j)
        gram = lax.dot_general(v, v, TN, preferred_element_type=F32)
        g1, g2, g3 = split3(gram)
        gsplit[j, 0] = g1.astype(BF16)
        gsplit[j, 1] = g2.astype(BF16)
        gsplit[j, 2] = g3.astype(BF16)
        seed = seed_ref[j].astype(F32)
        lhs = jnp.concatenate([seed, jnp.zeros_like(seed)], axis=0).astype(BF16)
        acc = jnp.dot(lhs, gsplit[j, 2], preferred_element_type=F32)
        acc = acc + jnp.dot(lhs, gsplit[j, 1], preferred_element_type=F32)
        acc = acc + jnp.dot(lhs, gsplit[j, 0], preferred_element_type=F32)
        first.append(acc[:rank])
    ybuf[0, my_chan] = jnp.concatenate(first, axis=0)
    pl.semaphore_wait(barrier, n_all - 1)
    push(ybuf.at[0], my_chan, n_chan, along_chan, 0)

    lmp[...] = jnp.zeros_like(lmp)
    lmp[0:dirs, :] = lm_ref[...]
    tbp[...] = jnp.zeros_like(tbp)
    tbp[0:dirs, :] = tb_ref[...]
    clp[...] = jnp.full_like(clp, -1)
    clp[0:1, 0:dirs] = cluster_ref[...]
    c1, c2, c3 = split3(coords_ref[...])
    coord_rows[...] = jnp.zeros_like(coord_rows)
    coord_rows[0:2, :] = c1
    coord_rows[2:4, :] = c2
    coord_rows[4:6, :] = c3
    station = lax.broadcasted_iota(jnp.int32, (stations, base_dev), 0)
    pick = jnp.where(station == pair_ref[0:1, :], F32(1.0), F32(0.0)) - jnp.where(
        station == pair_ref[1:2, :], F32(1.0), F32(0.0)
    )
    uv_ref[...] = jnp.dot(coord_rows[...].astype(BF16), pick.astype(BF16), preferred_element_type=F32)
    uv = uv_ref[0:2, :] + uv_ref[2:4, :] + uv_ref[4:6, :]
    geo = lmp[:, 0:1] * uv[0:1, :] + lmp[:, 1:2] * uv[1:2, :]
    for c in range(chan_dev):
        chan = jnp.full((1, tile), my_chan * chan_dev + c, jnp.int32).astype(F32)
        scale = F32(PHASE_SCALE) * (F32(1.0) + chan / F32(channels))
        for j in range(tiles):
            cos, sin = sincos(scale * geo[:, j * tile : (j + 1) * tile])
            resp[j, :, c * tile : (c + 1) * tile] = cos.astype(BF16)
            resp[j, :, (chan_dev + c) * tile : (chan_dev + c + 1) * tile] = sin.astype(BF16)

    def advance(block, step):
        parts = []
        for j in range(tiles):
            z1, z2, z3 = split3(block[j])
            lhs = jnp.concatenate([z1, z2, z3, jnp.zeros_like(z1)], axis=0).astype(BF16)
            p1 = jnp.dot(lhs, gsplit[j, 0], preferred_element_type=F32)
            p2 = jnp.dot(lhs, gsplit[j, 1], preferred_element_type=F32)
            p3 = jnp.dot(lhs, gsplit[j, 2], preferred_element_type=F32)
            low = p1[2 * rank : 3 * rank] + p2[rank : 2 * rank] + p3[:rank]
            parts.append(p1[:rank] + (p1[rank : 2 * rank] + p2[:rank] + low))
        ybuf[step, my_chan] = jnp.concatenate(parts, axis=0)
        push(ybuf.at[step], my_chan, n_chan, along_chan, step)

    def gathered(step):
        arrived(ybuf.at[step], n_chan, step)
        return orthonormal(total(ybuf.at[step], n_chan).reshape(tiles, rank, times))

    advance(gathered(0), 1)

    tb = tbp[...]
    beam_gram = lax.dot_general(tb, tb, NT, precision=HIGHEST, preferred_element_type=F32)
    member = jnp.where(
        lax.broadcasted_iota(jnp.int32, (LANES, dpad), 0) == clp[0:1, 0:dpad], F32(1.0), F32(0.0)
    )
    member_rows = member[0:GROUP]
    halves = []
    for j in range(tiles):
        r = resp[j]
        model = lax.dot_general(r, r, NT, preferred_element_type=F32)
        halves.append(jnp.dot(member_rows, model * beam_gram, precision=HIGHEST, preferred_element_type=F32))
    half = jnp.concatenate(halves, axis=0)
    nbuf[my_chan] = lax.dot_general(half, member, NT, precision=HIGHEST, preferred_element_type=F32)
    push(nbuf, my_chan, n_chan, along_chan, SUB_ITERS)
    before = []
    for j in range(tiles):
        bp = jnp.dot(resp[j], vis_tile(j), preferred_element_type=F32)
        before.append(jnp.sum(bp * tb, axis=-1, keepdims=True))
        b1, b2, b3 = split3(bp)
        bsplit[j, 0] = b1.astype(BF16)
        bsplit[j, 1] = b2.astype(BF16)
        bsplit[j, 2] = b3.astype(BF16)
    b1, b2, b3 = split3(tb)
    bsplit[tiles, 0] = b1.astype(BF16)
    bsplit[tiles, 1] = b2.astype(BF16)
    bsplit[tiles, 2] = b3.astype(BF16)

    advance(gathered(1), 2)

    arrived(nbuf, n_chan, SUB_ITERS)
    normal = total(nbuf, n_chan)
    sub = lax.broadcasted_iota(jnp.int32, (GROUP, LANES), 0)
    lane = lax.broadcasted_iota(jnp.int32, (GROUP, LANES), 1)
    eye = jnp.where(sub == lane, F32(1.0), F32(0.0))
    inv, inv_rho = [], []
    for j in range(tiles):
        mat = normal[j * GROUP : (j + 1) * GROUP]
        trace = jnp.sum(jnp.sum(mat * eye, axis=1, keepdims=True), axis=0, keepdims=True)
        recip = F32(1.0) / (F32(RHO_SCALE) * trace / F32(CL))
        inv_rho.append(recip)
        inv.append(mat * recip + eye)
    for p in range(CL):
        for j in range(tiles):
            mat = inv[j]
            col = mat[:, p : p + 1]
            row = mat[p : p + 1, :]
            d = F32(1.0) / mat[p : p + 1, p : p + 1]
            row = jnp.where(lane[0:1] == p, d, row * d)
            mat = jnp.where(lane == p, F32(0.0), mat)
            inv[j] = jnp.where(sub == p, row, mat - col * row)
    big, start = [], []
    for j in range(tiles):
        e = eye - inv[j]
        a = inv[j] * inv_rho[j]
        if j:
            e = pltpu.roll(e, j * GROUP, 1)
            a = pltpu.roll(a, j * GROUP, 1)
        big.append(e)
        start.append(a)
    pad = jnp.zeros((LANES - tiles * GROUP, LANES), F32)
    e1 = jnp.concatenate(big + [pad], axis=0)
    a0 = jnp.concatenate(start + [pad], axis=0)

    def times_of(a, b):
        return jnp.dot(a, b, precision=HIGHEST, preferred_element_type=F32)

    def fold(m):
        out = m[0:GROUP]
        for j in range(1, tiles):
            out = out + m[j * GROUP : (j + 1) * GROUP]
        return out

    def fold_lanes(m):
        out = m
        for j in range(1, tiles):
            out = out + pltpu.roll(m, LANES - j * GROUP, 1)
        return jnp.where(lax.broadcasted_iota(jnp.int32, m.shape, 1) < GROUP, out, F32(0.0))

    e2 = times_of(e1, e1)
    e3 = times_of(e2, e1)
    e4 = times_of(e2, e2)
    e5 = times_of(e2, e3)
    powers = [fold(m) for m in (e1, e2, e3, e4, e5)]
    packed = fold_lanes(powers[0])
    for p in range(1, ADMM_ITERS - 1):
        packed = packed + pltpu.roll(fold_lanes(powers[p]), p * GROUP, 1)
    mbuf[my_bl] = packed
    push(mbuf, my_bl, n_bl, along_bl, SUB_ITERS + 1)
    series = [a0]
    for m in (e1, e2, e3, e4, e5):
        series.append(times_of(m, a0))
    series = [fold(m) for m in series]
    eye_all = jnp.where(lax.rem(lane, GROUP) == sub, F32(1.0), F32(0.0))
    eye_all = jnp.where(lane < tiles * GROUP, eye_all, F32(0.0))
    powers = [eye_all] + powers

    basis = gathered(2).astype(BF16).astype(F32).reshape(tiles * rank, times)
    basis_ref[...] = basis
    lhs = bsplit[...].reshape((tiles + 1) * 3 * dpad, times)
    coef = lax.dot_general(lhs, basis.astype(BF16), NT, preferred_element_type=F32)

    def joined(i):
        at = i * 3 * dpad
        return coef[at : at + dpad] + (coef[at + dpad : at + 2 * dpad] + coef[at + 2 * dpad : at + 3 * dpad])

    beam_coef = joined(tiles)
    col_lane = lax.broadcasted_iota(jnp.int32, (dpad, tiles * rank), 1)
    wide_lane = lax.broadcasted_iota(jnp.int32, (dpad, LANES), 1)
    cols = jnp.zeros((dpad, LANES), F32)
    for j in range(tiles):
        inside = (col_lane >= j * rank) & (col_lane < (j + 1) * rank)
        product = jnp.where(inside, joined(j) * beam_coef, F32(0.0))
        col = before[j] - jnp.sum(product, axis=-1, keepdims=True)
        here = (wide_lane >= j * GROUP) & (wide_lane < (j + 1) * GROUP)
        cols = jnp.where(here, col, cols)
    rhs = jnp.dot(member_rows, cols, precision=HIGHEST, preferred_element_type=F32)
    rows, run = [], None
    for m in range(ADMM_ITERS):
        row = jnp.sum(series[m] * rhs, axis=0, keepdims=True)
        run = row if m == 0 else run + row
        rows.append(run)
        last = row
    out_sub = lax.broadcasted_iota(jnp.int32, (8, LANES), 0)
    block = jnp.zeros((8, LANES), F32)
    for m in range(ADMM_ITERS):
        block = jnp.where(out_sub == m, rows[m], block)
    block = fold_lanes(block)
    vbuf[my_id] = jnp.where(out_sub == ADMM_ITERS, last, block)
    push(vbuf, my_id, n_all, everyone, SUB_ITERS + 2)

    arrived(mbuf, n_bl, SUB_ITERS + 1)
    moments = total(mbuf, n_bl) * F32(1.0 / tiles_all)
    history = [eye]
    for p in range(ADMM_ITERS - 1):
        m = moments if p == 0 else pltpu.roll(moments, LANES - p * GROUP, 1)
        history.append(jnp.where(lane < GROUP, m, F32(0.0)))
    gain = [history[p] - F32(2.0) * history[p + 1] for p in range(ADMM_ITERS - 1)]
    local = []
    for i in range(1, ADMM_ITERS - 1):
        k = ADMM_ITERS - 2 - i
        local.append(F32(3.0) * powers[k + 1] - powers[k] - F32(2.0) * powers[k + 2])
    local.append(F32(2.0) * (powers[0] - powers[1]))
    arrived(vbuf, n_all, SUB_ITERS + 2)
    sums = total(vbuf, n_all) * F32(1.0 / tiles_all)
    mine = vbuf[my_bl]
    for i in range(1, n_chan):
        mine = mine + vbuf[i * n_bl + my_bl]
    x = mine[ADMM_ITERS : ADMM_ITERS + 1]
    cols_z = []
    spread = jnp.zeros((GROUP, LANES), F32)
    for k in range(ADMM_ITERS):
        z = sums[k : k + 1]
        if k:
            acc = gain[k - 1] * cols_z[0]
            for i in range(1, k):
                acc = acc + gain[k - 1 - i] * cols_z[i]
            z = z + jnp.sum(acc, axis=0, keepdims=True)
        if k < ADMM_ITERS - 1:
            col = jnp.sum(eye * z, axis=1, keepdims=True)
            cols_z.append(col)
            spread = spread + local[k] * col
    x = x + jnp.sum(spread, axis=0, keepdims=True)
    factor = F32((channels * tile * times) ** 0.5)
    x = jnp.broadcast_to(x * factor, (8, LANES))
    for j in range(tiles):
        at = x if j == 0 else pltpu.roll(x, LANES - j * GROUP, 1)
        gains_ref[j : j + 1, :] = at[0:1, 0:CL]
    cons_ref[...] = (z * factor)[:, 0:CL]

    for step in range(SUB_ITERS):
        sent(ybuf.at[step], n_chan, step)
    sent(nbuf, n_chan, SUB_ITERS)
    sent(mbuf, n_bl, SUB_ITERS + 1)
    sent(vbuf, n_all, SUB_ITERS + 2)


def clean_kernel(vis_ref, basis_ref, out_ref):
    rank = basis_ref.shape[0]
    times = basis_ref.shape[1]
    basis = basis_ref[...]
    wide = jnp.concatenate([basis, basis, basis, jnp.zeros_like(basis)], axis=0).astype(BF16)
    v = vis_ref[...].reshape(-1, times)
    proj = lax.dot_general(v, wide, NT, preferred_element_type=F32)
    lane = lax.broadcasted_iota(jnp.int32, (1, 4 * rank), 1)
    a, b, c = split3(proj)
    parts = jnp.where(lane < rank, a, jnp.where(lane < 2 * rank, b, c)).astype(BF16)
    correction = jnp.dot(parts, wide, preferred_element_type=F32)
    out_ref[...] = (v.astype(F32) - correction).astype(BF16).reshape(out_ref.shape)


def per_device(vis, station_pair_index, station_coords, dir_lm, time_beam, dir_cluster, seed_block):
    n_chan = lax.axis_size("chan")
    n_bl = lax.axis_size("bl")
    chan_dev, base_dev, times = vis.shape[1:]
    tiles, _, rank = seed_block.shape
    tile = base_dev // tiles
    dirs = dir_lm.shape[0]
    dpad = (dirs + 15) // 16 * 16
    stations = station_coords.shape[0]
    vmem = pl.BlockSpec(memory_space=pltpu.VMEM)
    basis, gains, consensus = pl.pallas_call(
        functools.partial(main_kernel, n_chan, n_bl, chan_dev * n_chan),
        out_shape=(
            jax.ShapeDtypeStruct((tiles * rank, times), F32),
            jax.ShapeDtypeStruct((tiles, CL), F32),
            jax.ShapeDtypeStruct((1, CL), F32),
        ),
        in_specs=[vmem] * 7,
        out_specs=(vmem,) * 3,
        scratch_shapes=[
            pltpu.VMEM((tiles, 3, times, times), BF16),
            pltpu.VMEM((tiles, dpad, 2 * chan_dev * tile), BF16),
            pltpu.VMEM((dpad, 2), F32),
            pltpu.VMEM((dpad, times), F32),
            pltpu.VMEM((8, LANES), jnp.int32),
            pltpu.VMEM((GROUP, stations), F32),
            pltpu.VMEM((GROUP, base_dev), F32),
            pltpu.VMEM((8, LANES), F32),
            pltpu.VMEM((tiles + 1, 3, dpad, times), BF16),
            pltpu.VMEM((SUB_ITERS, n_chan, tiles * rank, times), F32),
            pltpu.VMEM((n_chan, tiles * GROUP, LANES), F32),
            pltpu.VMEM((n_bl, GROUP, LANES), F32),
            pltpu.VMEM((n_chan * n_bl, 8, LANES), F32),
            pltpu.SemaphoreType.DMA((SUB_ITERS + 3,)),
            pltpu.SemaphoreType.DMA((SUB_ITERS + 3,)),
        ],
        compiler_params=pltpu.CompilerParams(
            collective_id=0, has_side_effects=True, vmem_limit_bytes=48 * 1024 * 1024
        ),
    )(
        vis,
        station_pair_index.T,
        station_coords.T,
        dir_lm,
        time_beam,
        dir_cluster.reshape(1, dirs),
        jnp.swapaxes(seed_block, 1, 2),
    )
    spec = pl.BlockSpec((2, chan_dev, tile, times), lambda j: (0, 0, j, 0))
    clean = pl.pallas_call(
        clean_kernel,
        grid=(tiles,),
        out_shape=jax.ShapeDtypeStruct(vis.shape, BF16),
        in_specs=[spec, pl.BlockSpec((rank, times), lambda j: (j, 0))],
        out_specs=spec,
        compiler_params=pltpu.CompilerParams(vmem_limit_bytes=32 * 1024 * 1024),
    )(vis, basis)
    return clean, gains, consensus.reshape(CL)


def solution(mesh):
    placed = (P(None, "chan", "bl", None), P("bl", None), P(), P(), P(), P(), P("bl", None, None))
    return jax.shard_map(
        per_device,
        mesh=mesh,
        in_specs=placed,
        out_specs=(P(None, "chan", "bl", None), P("bl", None), P()),
        check_vma=False,
    )
```

time: 302 us -> 35.3 us (0.12)
  blocking collectives: 188 us -> 0 us
  other arithmetic: 40.2 us -> 0 us
  waiting for transfers between devices: 34.6 us -> 0 us
  Pallas kernels: 0 us -> 27.2 us
  matrix products: 22.6 us -> 0 us
  between operations: 14.2 us -> 0.65 us
  local copies, waits for them, and re-layouts: 1.88 us -> 7.08 us
    psum x7 -> x0, blocking collectives: 188 us -> none  [the longest x6 179 us: consensus_total(): return lax.psum(values, 'bl')]
    another operation x25 -> x0, other arithmetic: 36.6 us -> none  [the longest x10 13.2 us: orthonormal(): lower = jnp.linalg.cholesky(square)]
    psum x1 -> x0, waiting for transfers between devices: 34.6 us -> none  [per_device(): gram = lax.psum(gram_part, 'chan')]
    pallas_call x0 -> x2, Pallas kernels: none -> 27.2 us  [the longest x1 23.9 us: per_device(): pl.pallas_call(functools.partial(main_kernel, n_chan, n_bl, chan_dev * n_...]
    dot_general x19 -> x0, matrix products: 19.8 us -> none  [the longest x3 5.47 us: per_device(): jnp.einsum('jts,jsk->jtk', gram, block, precision=HIGHEST)]
    unnamed x14 -> x15, local copies, waits for them, and re-layouts: 0.03 us -> 7.08 us
  transfers between devices with their start and end apart: 1 -> 0, of which waited for: 1 -> 0; matrix products, arithmetic and copies ran while one was open for 3% -> 0% of each run, Pallas kernels for 0% -> 0%
where the time goes in v1:
time: 35.3 us; the launch traced here: 35 us
  Pallas kernels  27.2 us (77%)
  local copies, waits for them, and re-layouts  7.08 us (20%)
  between operations  0.65 us (2%)
    pallas_call x1, Pallas kernels, per_device(): pl.pallas_call(functools.partial(main_kernel, n_chan, n_bl, chan_dev * n_...  23.9 us
    unnamed x15, local copies, waits for them, and re-layouts  7.08 us
    pallas_call x1, Pallas kernels, per_device(): pl.pallas_call(clean_kernel, grid=(tiles,), out_shape=jax.ShapeDtypeStruc...  3.32 us

profile of v1, /device:TPU:0, one launch (start us, length us, event | category | flops | bytes accessed | tf_op | source)
XLA Modules:
  0.0 35.0 jit_solution(10239422401493248396)
XLA Ops:
  0.6 0.8 %copy.10.lm_ref = f32[60,2]{1,0:T(8,128)S(1)} copy(f32[60,2]{0,1:T(2,128)} %param.10) | data formatting | bytes 960 | tf_op args[3]
  1.4 0.0 copy-start
  1.4 1.6 %copy-done = bf16[2,4,512,256]{3,2,1,0:T(8,128)(2,1)S(1)} copy-done((bf16[2,4,512,256]{3,2,1,0:T(8,128)(2,1)S(1)}, bf16[2,4,512,256]{3,2,1,0:T(8,128)(2,1)}, u32[]{:S(2)}) %copy-start) | copy-done | bytes 2097176
  3.0 0.0 copy-start.1
  3.0 0.8 %copy-done.1 = f32[60,256]{1,0:T(8,128)S(1)} copy-done((f32[60,256]{1,0:T(8,128)S(1)}, f32[60,256]{1,0:T(8,128)}, u32[]{:S(2)}) %copy-start.1) | copy-done | bytes 61464
  3.8 0.0 copy-start.2
  3.8 0.8 %copy-done.2 = s32[4,256,8]{1,2,0:T(8,128)S(1)} copy-done((s32[4,256,8]{1,2,0:T(8,128)S(1)}, s32[4,256,8]{1,2,0:T(8,128)}, u32[]{:S(2)}) %copy-start.2) | copy-done | bytes 32792
  4.6 0.0 copy-start.3
  4.6 0.7 %copy-done.3 = s32[512,2]{0,1:T(2,128)S(1)} copy-done((s32[512,2]{0,1:T(2,128)S(1)}, s32[512,2]{0,1:T(2,128)}, u32[]{:S(2)}) %copy-start.3) | copy-done | bytes 4120
  5.3 0.0 copy-start.4
  5.3 0.7 %copy-done.4 = f32[512,2]{0,1:T(2,128)S(1)} copy-done((f32[512,2]{0,1:T(2,128)S(1)}, f32[512,2]{0,1:T(2,128)}, u32[]{:S(2)}) %copy-start.4) | copy-done | bytes 4120
  6.0 0.0 copy-start.5
  6.0 0.7 %copy-done.5 = s32[60]{0:T(128)S(1)} copy-done((s32[60]{0:T(128)S(1)}, s32[60]{0:T(128)}, u32[]{:S(2)}) %copy-start.5) | copy-done | bytes 264
  6.6 23.9 %shard_map.94 = (f32[32,256]{1,0:T(8,128)S(1)}, f32[4,12]{1,0:T(4,128)S(1)}, f32[1,12]{1,0:T(1,128)S(1)}) custom-call(bf16[2,4,512,256]{3,2,1,0:T(8,128)(2,1)S(1)} %copy-done, s32[2,512]{1,0:T(2,128)S(1)} %bitcast.6, f32[2,512]{1,0:T(2,128)S(1)} %bitcast.7, f32[60,2]{1,0:T(8,128)S(1)} %copy.10.lm_ref, f32[60,256]{1,0:T(8,128)S(1)} %copy-done.1, ...), custom_call_target="tpu_custom_call" | custom-call | tf_op jit(solution)/shard_map/pallas_call | solution.py:391
  30.6 3.3 %shard_map.95 = bf16[2,4,512,256]{3,2,1,0:T(8,128)(2,1)} custom-call(bf16[2,4,512,256]{3,2,1,0:T(8,128)(2,1)S(1)} %copy-done, f32[32,256]{1,0:T(8,128)S(1)} %get-tuple-element.6.basis_ref), custom_call_target="tpu_custom_call" | custom-call | tf_op jit(solution)/shard_map/pallas_call | solution.py:430
  33.9 0.6 %copy.13 = f32[4,12]{1,0:T(4,128)} copy(f32[4,12]{1,0:T(4,128)S(1)} %get-tuple-element.13) | data formatting | bytes 384
  34.5 0.5 %copy.14 = f32[12]{0:T(128)} copy(f32[12]{0:T(128)S(1)} %bitcast.9) | data formatting | bytes 96
Async XLA Ops:
  1.4 1.6 %copy-start = (bf16[2,4,512,256]{3,2,1,0:T(8,128)(2,1)S(1)}, bf16[2,4,512,256]{3,2,1,0:T(8,128)(2,1)}, u32[]{:S(2)}) copy-start(bf16[2,4,512,256]{3,2,1,0:T(8,128)(2,1)} %vis_ref.3) | copy-start | bytes 6291460
  3.0 0.8 %copy-start.1 = (f32[60,256]{1,0:T(8,128)S(1)}, f32[60,256]{1,0:T(8,128)}, u32[]{:S(2)}) copy-start(f32[60,256]{1,0:T(8,128)} %tb_ref.1) | copy-start | bytes 184324
  3.8 0.8 %copy-start.2 = (s32[4,256,8]{1,2,0:T(8,128)S(1)}, s32[4,256,8]{1,2,0:T(8,128)}, u32[]{:S(2)}) copy-start(s32[4,256,8]{1,2,0:T(8,128)} %param.13) | copy-start | bytes 98308
  4.6 0.7 %copy-start.3 = (s32[512,2]{0,1:T(2,128)S(1)}, s32[512,2]{0,1:T(2,128)}, u32[]{:S(2)}) copy-start(s32[512,2]{0,1:T(2,128)} %param.8) | copy-start | bytes 12292
  5.3 0.7 %copy-start.4 = (f32[512,2]{0,1:T(2,128)S(1)}, f32[512,2]{0,1:T(2,128)}, u32[]{:S(2)}) copy-start(f32[512,2]{0,1:T(2,128)} %param.9) | copy-start | bytes 12292
  6.0 0.7 %copy-start.5 = (s32[60]{0:T(128)S(1)}, s32[60]{0:T(128)}, u32[]{:S(2)}) copy-start(s32[60]{0:T(128)} %param.12) | copy-start | bytes 724

commit v2 on v1

--- a/solution.py
+++ b/solution.py
@@ -63,22 +63,46 @@
 
 def main_kernel(
     n_chan, n_bl, channels,
+    vis_hbm, pair_hbm, coords_hbm, lm_hbm, tb_hbm, cluster_hbm, seed_hbm,
+    basis_ref, gains_ref, cons_ref,
     vis_ref, pair_ref, coords_ref, lm_ref, tb_ref, cluster_ref, seed_ref,
-    basis_ref, gains_ref, cons_ref,
-    gsplit, resp, lmp, tbp, clp, coord_rows, uv_ref, beam, bsplit,
-    ybuf, nbuf, mbuf, vbuf, send_sems, recv_sems,
+    gsplit, resp, lmp, tbp, clp, coord_rows, uv_ref, bsplit,
+    ybuf, nbuf, mbuf, vbuf, send_sems, recv_sems, vis_sems, load_sems,
 ):
     chan_dev, base_dev, times = vis_ref.shape[1:]
     tiles, rank = seed_ref.shape[0], seed_ref.shape[1]
     tile = base_dev // tiles
-    dirs = lm_ref.shape[0]
-    dpad = lmp.shape[0]
+    dirs = tb_ref.shape[0]
+    dpad = tbp.shape[0]
     stations = coords_ref.shape[1]
     n_all = n_chan * n_bl
     tiles_all = tiles * n_bl
     my_chan = lax.axis_index("chan")
     my_bl = lax.axis_index("bl")
     my_id = my_chan * n_bl + my_bl
+
+    loads = [
+        pltpu.make_async_copy(src, dst, load_sems.at[i])
+        for i, (src, dst) in enumerate(
+            (
+                (seed_hbm, seed_ref),
+                (pair_hbm, pair_ref),
+                (coords_hbm, coords_ref),
+                (lm_hbm, lm_ref),
+                (tb_hbm, tb_ref),
+                (cluster_hbm, cluster_ref),
+            )
+        )
+    ]
+    vis_loads = []
+    for j in range(tiles):
+        at = (slice(None), slice(None), pl.ds(j * tile, tile), slice(None))
+        vis_loads.append(pltpu.make_async_copy(vis_hbm.at[at], vis_ref.at[at], vis_sems.at[j]))
+    loads[0].start()
+    for load in vis_loads:
+        load.start()
+    for load in loads[1:]:
+        load.start()
 
     def everyone(off):
         other = lax.rem(my_id + off, n_all)
@@ -126,7 +150,9 @@
         return vis_ref[:, :, j * tile : (j + 1) * tile, :].reshape(2 * chan_dev * tile, times)
 
     first = []
-    for j in range(tiles):
+    loads[0].wait()
+    for j in range(tiles):
+        vis_loads[j].wait()
         v = vis_tile(j)
         gram = lax.dot_general(v, v, TN, preferred_element_type=F32)
         g1, g2, g3 = split3(gram)
@@ -143,8 +169,10 @@
     pl.semaphore_wait(barrier, n_all - 1)
     push(ybuf.at[0], my_chan, n_chan, along_chan, 0)
 
+    for load in loads[1:]:
+        load.wait()
     lmp[...] = jnp.zeros_like(lmp)
-    lmp[0:dirs, :] = lm_ref[...]
+    lmp[0:2, 0:dirs] = lm_ref[...]
     tbp[...] = jnp.zeros_like(tbp)
     tbp[0:dirs, :] = tb_ref[...]
     clp[...] = jnp.full_like(clp, -1)
@@ -160,7 +188,11 @@
     )
     uv_ref[...] = jnp.dot(coord_rows[...].astype(BF16), pick.astype(BF16), preferred_element_type=F32)
     uv = uv_ref[0:2, :] + uv_ref[2:4, :] + uv_ref[4:6, :]
-    geo = lmp[:, 0:1] * uv[0:1, :] + lmp[:, 1:2] * uv[1:2, :]
+    uv_ref[0:2, :] = uv
+    uv_ref[2:8, :] = jnp.zeros((6, base_dev), F32)
+    geo = lax.dot_general(
+        lmp[:, 0:dpad], uv_ref[0:8, :], TN, precision=HIGHEST, preferred_element_type=F32
+    )
     for c in range(chan_dev):
         chan = jnp.full((1, tile), my_chan * chan_dev + c, jnp.int32).astype(F32)
         scale = F32(PHASE_SCALE) * (F32(1.0) + chan / F32(channels))
@@ -364,7 +396,9 @@
     sent(vbuf, n_all, SUB_ITERS + 2)
 
 
-def clean_kernel(vis_ref, basis_ref, out_ref):
+def clean_kernel(vis_ref, basis_ref, gains_in, cons_in, out_ref, gains_ref, cons_ref):
+    gains_ref[...] = gains_in[...]
+    cons_ref[...] = cons_in[...]
     rank = basis_ref.shape[0]
     times = basis_ref.shape[1]
     basis = basis_ref[...]
@@ -395,17 +429,23 @@
             jax.ShapeDtypeStruct((tiles, CL), F32),
             jax.ShapeDtypeStruct((1, CL), F32),
         ),
-        in_specs=[vmem] * 7,
+        in_specs=[pl.BlockSpec(memory_space=pl.ANY)] * 7,
         out_specs=(vmem,) * 3,
         scratch_shapes=[
+            pltpu.VMEM(vis.shape, BF16),
+            pltpu.VMEM((2, base_dev), jnp.int32),
+            pltpu.VMEM((2, stations), F32),
+            pltpu.VMEM((2, dirs), F32),
+            pltpu.VMEM((dirs, times), F32),
+            pltpu.VMEM((1, dirs), jnp.int32),
+            pltpu.VMEM((tiles, rank, times), jnp.int32),
             pltpu.VMEM((tiles, 3, times, times), BF16),
             pltpu.VMEM((tiles, dpad, 2 * chan_dev * tile), BF16),
-            pltpu.VMEM((dpad, 2), F32),
+            pltpu.VMEM((8, LANES), F32),
             pltpu.VMEM((dpad, times), F32),
             pltpu.VMEM((8, LANES), jnp.int32),
             pltpu.VMEM((GROUP, stations), F32),
             pltpu.VMEM((GROUP, base_dev), F32),
-            pltpu.VMEM((8, LANES), F32),
             pltpu.VMEM((tiles + 1, 3, dpad, times), BF16),
             pltpu.VMEM((SUB_ITERS, n_chan, tiles * rank, times), F32),
             pltpu.VMEM((n_chan, tiles * GROUP, LANES), F32),
@@ -413,28 +453,36 @@
             pltpu.VMEM((n_chan * n_bl, 8, LANES), F32),
             pltpu.SemaphoreType.DMA((SUB_ITERS + 3,)),
             pltpu.SemaphoreType.DMA((SUB_ITERS + 3,)),
+            pltpu.SemaphoreType.DMA((tiles,)),
+            pltpu.SemaphoreType.DMA((6,)),
         ],
         compiler_params=pltpu.CompilerParams(
-            collective_id=0, has_side_effects=True, vmem_limit_bytes=48 * 1024 * 1024
+            collective_id=0, has_side_effects=True, vmem_limit_bytes=60 * 1024 * 1024
         ),
     )(
         vis,
         station_pair_index.T,
         station_coords.T,
-        dir_lm,
+        dir_lm.T,
         time_beam,
         dir_cluster.reshape(1, dirs),
         jnp.swapaxes(seed_block, 1, 2),
     )
     spec = pl.BlockSpec((2, chan_dev, tile, times), lambda j: (0, 0, j, 0))
-    clean = pl.pallas_call(
+    gains_spec = pl.BlockSpec((tiles, CL), lambda j: (0, 0))
+    cons_spec = pl.BlockSpec((1, CL), lambda j: (0, 0))
+    clean, gains, consensus = pl.pallas_call(
         clean_kernel,
         grid=(tiles,),
-        out_shape=jax.ShapeDtypeStruct(vis.shape, BF16),
-        in_specs=[spec, pl.BlockSpec((rank, times), lambda j: (j, 0))],
-        out_specs=spec,
-        compiler_params=pltpu.CompilerParams(vmem_limit_bytes=32 * 1024 * 1024),
-    )(vis, basis)
+        out_shape=(
+            jax.ShapeDtypeStruct(vis.shape, BF16),
+            jax.ShapeDtypeStruct((tiles, CL), F32),
+            jax.ShapeDtypeStruct((1, CL), F32),
+        ),
+        in_specs=[spec, pl.BlockSpec((rank, times), lambda j: (j, 0)), gains_spec, cons_spec],
+        out_specs=(spec, gains_spec, cons_spec),
+        compiler_params=pltpu.CompilerParams(vmem_limit_bytes=60 * 1024 * 1024),
+    )(vis, basis, gains, consensus)
     return clean, gains, consensus.reshape(CL)
 
 

time: 35.3 us -> 31.5 us (0.89)
  local copies, waits for them, and re-layouts: 7.08 us -> 0 us
  Pallas kernels: 27.2 us -> 30.7 us
    unnamed x15 -> x0, local copies, waits for them, and re-layouts: 7.08 us -> none
    pallas_call x1, Pallas kernels: 23.9 us -> 25.9 us  [per_device(): pl.pallas_call(functools.partial(main_kernel, n_chan, n_bl, chan_dev * n_...]
    pallas_call x1, Pallas kernels: 3.32 us -> 4.79 us  [per_device(): pl.pallas_call(clean_kernel, grid=(tiles,), out_shape=(jax.ShapeDtypeStru...]
where the time goes in v2:
time: 31.5 us; the launch traced here: 31.3 us
  Pallas kernels  30.7 us (97%)
  between operations  0.64 us (2%)
    pallas_call x1, Pallas kernels, per_device(): pl.pallas_call(functools.partial(main_kernel, n_chan, n_bl, chan_dev * n_...  25.9 us
    pallas_call x1, Pallas kernels, per_device(): pl.pallas_call(clean_kernel, grid=(tiles,), out_shape=(jax.ShapeDtypeStru...  4.79 us

profile of v2, /device:TPU:0, one launch (start us, length us, event | category | flops | bytes accessed | tf_op | source)
XLA Modules:
  0.0 31.3 jit_solution(15316786176898980310)
XLA Ops:
  0.6 25.9 %shard_map.94 = (f32[32,256]{1,0:T(8,128)}, f32[4,12]{1,0:T(4,128)}, f32[1,12]{1,0:T(1,128)}) custom-call(bf16[2,4,512,256]{3,2,1,0:T(8,128)(2,1)} %vis_ref.1, s32[2,512]{1,0:T(2,128)} %bitcast.7, f32[2,512]{1,0:T(2,128)} %bitcast.8, f32[2,60]{1,0:T(2,128)} %bitcast.9, f32[60,256]{1,0:T(8,128)} %tb_hbm.1, s32[1,60]{1,0:T(1,128)} %bitcast.10, ...), custom_call_target="tpu_custom_call" | custom-call | tf_op jit(solution)/shard_map/pallas_call | solution.py:425
  26.5 4.8 %shard_map.95 = (bf16[2,4,512,256]{3,2,1,0:T(8,128)(2,1)}, f32[4,12]{1,0:T(4,128)}, f32[1,12]{1,0:T(1,128)}) custom-call(bf16[2,4,512,256]{3,2,1,0:T(8,128)(2,1)} %vis_ref.1, f32[32,256]{1,0:T(8,128)} %get-tuple-element.9.basis_ref, f32[4,12]{1,0:T(4,128)} %get-tuple-element.10.gains_in, f32[1,12]{1,0:T(1,128)} %get-tuple-element.11.cons_in), custom_call_target="tpu_custom_call" | custom-call | tf_op jit(solution)/shard_map/pallas_call | solution.py:474

commit v3 on v2

--- a/solution.py
+++ b/solution.py
@@ -50,13 +50,20 @@
 
 
 def orthonormal(rows):
-    sub = lax.broadcasted_iota(jnp.int32, (1, rows.shape[1], 1), 1)
-    for k in range(rows.shape[1]):
+    count = rows.shape[1]
+    sub = lax.broadcasted_iota(jnp.int32, (1, count, 1), 1)
+    for k in range(0, count, 2):
         lead = rows[:, k : k + 1, :]
+        follow = rows[:, k + 1 : k + 2, :]
         dots = jnp.sum(rows * lead, axis=-1, keepdims=True)
-        if k + 1 < rows.shape[1]:
-            coef = jnp.where(sub > k, dots / dots[:, k : k + 1, :], F32(0.0))
-            rows = rows - coef * lead
+        others = jnp.sum(rows * follow, axis=-1, keepdims=True)
+        ratio = dots / dots[:, k : k + 1, :]
+        mix = ratio[:, k + 1 : k + 2, :]
+        follow = follow - mix * lead
+        others = others - mix * dots
+        coef = jnp.where(sub > k, ratio, F32(0.0))
+        coef_follow = jnp.where(sub > k + 1, others / others[:, k + 1 : k + 2, :], F32(0.0))
+        rows = rows - coef * lead - coef_follow * follow
     norm = jnp.sum(rows * rows, axis=-1, keepdims=True)
     return rows / jnp.sqrt(norm)
 
@@ -64,10 +71,10 @@
 def main_kernel(
     n_chan, n_bl, channels,
     vis_hbm, pair_hbm, coords_hbm, lm_hbm, tb_hbm, cluster_hbm, seed_hbm,
-    basis_ref, gains_ref, cons_ref,
-    vis_ref, pair_ref, coords_ref, lm_ref, tb_ref, cluster_ref, seed_ref,
+    clean_hbm, gains_ref, cons_ref,
+    clean_ref, vis_ref, pair_ref, coords_ref, lm_ref, tb_ref, cluster_ref, seed_ref,
     gsplit, resp, lmp, tbp, clp, coord_rows, uv_ref, bsplit,
-    ybuf, nbuf, mbuf, vbuf, send_sems, recv_sems, vis_sems, load_sems,
+    ybuf, nbuf, mbuf, vbuf, send_sems, recv_sems, vis_sems, load_sems, clean_sems,
 ):
     chan_dev, base_dev, times = vis_ref.shape[1:]
     tiles, rank = seed_ref.shape[0], seed_ref.shape[1]
@@ -182,6 +189,11 @@
     coord_rows[0:2, :] = c1
     coord_rows[2:4, :] = c2
     coord_rows[4:6, :] = c3
+    tb = tbp[...]
+    beam_gram = lax.dot_general(tb, tb, NT, precision=HIGHEST, preferred_element_type=F32)
+    member = jnp.where(
+        lax.broadcasted_iota(jnp.int32, (LANES, dpad), 0) == clp[0:1, 0:dpad], F32(1.0), F32(0.0)
+    )
     station = lax.broadcasted_iota(jnp.int32, (stations, base_dev), 0)
     pick = jnp.where(station == pair_ref[0:1, :], F32(1.0), F32(0.0)) - jnp.where(
         station == pair_ref[1:2, :], F32(1.0), F32(0.0)
@@ -220,11 +232,6 @@
 
     advance(gathered(0), 1)
 
-    tb = tbp[...]
-    beam_gram = lax.dot_general(tb, tb, NT, precision=HIGHEST, preferred_element_type=F32)
-    member = jnp.where(
-        lax.broadcasted_iota(jnp.int32, (LANES, dpad), 0) == clp[0:1, 0:dpad], F32(1.0), F32(0.0)
-    )
     member_rows = member[0:GROUP]
     halves = []
     for j in range(tiles):
@@ -234,19 +241,6 @@
     half = jnp.concatenate(halves, axis=0)
     nbuf[my_chan] = lax.dot_general(half, member, NT, precision=HIGHEST, preferred_element_type=F32)
     push(nbuf, my_chan, n_chan, along_chan, SUB_ITERS)
-    before = []
-    for j in range(tiles):
-        bp = jnp.dot(resp[j], vis_tile(j), preferred_element_type=F32)
-        before.append(jnp.sum(bp * tb, axis=-1, keepdims=True))
-        b1, b2, b3 = split3(bp)
-        bsplit[j, 0] = b1.astype(BF16)
-        bsplit[j, 1] = b2.astype(BF16)
-        bsplit[j, 2] = b3.astype(BF16)
-    b1, b2, b3 = split3(tb)
-    bsplit[tiles, 0] = b1.astype(BF16)
-    bsplit[tiles, 1] = b2.astype(BF16)
-    bsplit[tiles, 2] = b3.astype(BF16)
-
     advance(gathered(1), 2)
 
     arrived(nbuf, n_chan, SUB_ITERS)
@@ -270,18 +264,27 @@
             row = jnp.where(lane[0:1] == p, d, row * d)
             mat = jnp.where(lane == p, F32(0.0), mat)
             inv[j] = jnp.where(sub == p, row, mat - col * row)
-    big, start = [], []
+    before = []
+    for j in range(tiles):
+        bp = jnp.dot(resp[j], vis_tile(j), preferred_element_type=F32)
+        before.append(jnp.sum(bp * tb, axis=-1, keepdims=True))
+        b1, b2, b3 = split3(bp)
+        bsplit[j, 0] = b1.astype(BF16)
+        bsplit[j, 1] = b2.astype(BF16)
+        bsplit[j, 2] = b3.astype(BF16)
+    b1, b2, b3 = split3(tb)
+    bsplit[tiles, 0] = b1.astype(BF16)
+    bsplit[tiles, 1] = b2.astype(BF16)
+    bsplit[tiles, 2] = b3.astype(BF16)
+
+    big = []
     for j in range(tiles):
         e = eye - inv[j]
-        a = inv[j] * inv_rho[j]
         if j:
             e = pltpu.roll(e, j * GROUP, 1)
-            a = pltpu.roll(a, j * GROUP, 1)
         big.append(e)
-        start.append(a)
     pad = jnp.zeros((LANES - tiles * GROUP, LANES), F32)
     e1 = jnp.concatenate(big + [pad], axis=0)
-    a0 = jnp.concatenate(start + [pad], axis=0)
 
     def times_of(a, b):
         return jnp.dot(a, b, precision=HIGHEST, preferred_element_type=F32)
@@ -302,22 +305,18 @@
     e3 = times_of(e2, e1)
     e4 = times_of(e2, e2)
     e5 = times_of(e2, e3)
-    powers = [fold(m) for m in (e1, e2, e3, e4, e5)]
+    e6 = times_of(e3, e3)
+    powers = [fold(m) for m in (e1, e2, e3, e4, e5, e6)]
     packed = fold_lanes(powers[0])
     for p in range(1, ADMM_ITERS - 1):
         packed = packed + pltpu.roll(fold_lanes(powers[p]), p * GROUP, 1)
     mbuf[my_bl] = packed
     push(mbuf, my_bl, n_bl, along_bl, SUB_ITERS + 1)
-    series = [a0]
-    for m in (e1, e2, e3, e4, e5):
-        series.append(times_of(m, a0))
-    series = [fold(m) for m in series]
     eye_all = jnp.where(lax.rem(lane, GROUP) == sub, F32(1.0), F32(0.0))
     eye_all = jnp.where(lane < tiles * GROUP, eye_all, F32(0.0))
     powers = [eye_all] + powers
 
     basis = gathered(2).astype(BF16).astype(F32).reshape(tiles * rank, times)
-    basis_ref[...] = basis
     lhs = bsplit[...].reshape((tiles + 1) * 3 * dpad, times)
     coef = lax.dot_general(lhs, basis.astype(BF16), NT, preferred_element_type=F32)
 
@@ -334,14 +333,12 @@
         product = jnp.where(inside, joined(j) * beam_coef, F32(0.0))
         col = before[j] - jnp.sum(product, axis=-1, keepdims=True)
         here = (wide_lane >= j * GROUP) & (wide_lane < (j + 1) * GROUP)
-        cols = jnp.where(here, col, cols)
+        cols = jnp.where(here, col * inv_rho[j], cols)
     rhs = jnp.dot(member_rows, cols, precision=HIGHEST, preferred_element_type=F32)
-    rows, run = [], None
-    for m in range(ADMM_ITERS):
-        row = jnp.sum(series[m] * rhs, axis=0, keepdims=True)
-        run = row if m == 0 else run + row
-        rows.append(run)
-        last = row
+    rows = [
+        jnp.sum((powers[0] - powers[m]) * rhs, axis=0, keepdims=True) for m in range(1, ADMM_ITERS + 1)
+    ]
+    last = jnp.sum((powers[ADMM_ITERS - 1] - powers[ADMM_ITERS]) * rhs, axis=0, keepdims=True)
     out_sub = lax.broadcasted_iota(jnp.int32, (8, LANES), 0)
     block = jnp.zeros((8, LANES), F32)
     for m in range(ADMM_ITERS):
@@ -349,6 +346,23 @@
     block = fold_lanes(block)
     vbuf[my_id] = jnp.where(out_sub == ADMM_ITERS, last, block)
     push(vbuf, my_id, n_all, everyone, SUB_ITERS + 2)
+
+    clean_stores = []
+    part_lane = lax.broadcasted_iota(jnp.int32, (1, 4 * rank), 1)
+    for j in range(tiles):
+        own = basis[j * rank : (j + 1) * rank]
+        wide = jnp.concatenate([own, own, own, jnp.zeros_like(own)], axis=0).astype(BF16)
+        v = vis_tile(j)
+        proj = lax.dot_general(v, wide, NT, preferred_element_type=F32)
+        a, b, c = split3(proj)
+        parts = jnp.where(part_lane < rank, a, jnp.where(part_lane < 2 * rank, b, c)).astype(BF16)
+        correction = jnp.dot(parts, wide, preferred_element_type=F32)
+        clean_ref[:, :, j * tile : (j + 1) * tile, :] = (
+            (v.astype(F32) - correction).astype(BF16).reshape(2, chan_dev, tile, times)
+        )
+        at = (slice(None), slice(None), pl.ds(j * tile, tile), slice(None))
+        clean_stores.append(pltpu.make_async_copy(clean_ref.at[at], clean_hbm.at[at], clean_sems.at[j]))
+        clean_stores[-1].start()
 
     arrived(mbuf, n_bl, SUB_ITERS + 1)
     moments = total(mbuf, n_bl) * F32(1.0 / tiles_all)
@@ -389,6 +403,8 @@
         gains_ref[j : j + 1, :] = at[0:1, 0:CL]
     cons_ref[...] = (z * factor)[:, 0:CL]
 
+    for store in clean_stores:
+        store.wait()
     for step in range(SUB_ITERS):
         sent(ybuf.at[step], n_chan, step)
     sent(nbuf, n_chan, SUB_ITERS)
@@ -396,20 +412,19 @@
     sent(vbuf, n_all, SUB_ITERS + 2)
 
 
-def clean_kernel(vis_ref, basis_ref, gains_in, cons_in, out_ref, gains_ref, cons_ref):
-    gains_ref[...] = gains_in[...]
-    cons_ref[...] = cons_in[...]
-    rank = basis_ref.shape[0]
-    times = basis_ref.shape[1]
-    basis = basis_ref[...]
-    wide = jnp.concatenate([basis, basis, basis, jnp.zeros_like(basis)], axis=0).astype(BF16)
-    v = vis_ref[...].reshape(-1, times)
-    proj = lax.dot_general(v, wide, NT, preferred_element_type=F32)
-    lane = lax.broadcasted_iota(jnp.int32, (1, 4 * rank), 1)
-    a, b, c = split3(proj)
-    parts = jnp.where(lane < rank, a, jnp.where(lane < 2 * rank, b, c)).astype(BF16)
-    correction = jnp.dot(parts, wide, preferred_element_type=F32)
-    out_ref[...] = (v.astype(F32) - correction).astype(BF16).reshape(out_ref.shape)
+def copy_kernel(clean_in, gains_in, cons_in, clean_out, gains_out, cons_out, sems):
+    parts, chans = clean_in.shape[:2]
+    copies = [
+        pltpu.make_async_copy(clean_in.at[p, c], clean_out.at[p, c], sems.at[p * chans + c])
+        for p in range(parts)
+        for c in range(chans)
+    ]
+    copies.append(pltpu.make_async_copy(gains_in, gains_out, sems.at[parts * chans]))
+    copies.append(pltpu.make_async_copy(cons_in, cons_out, sems.at[parts * chans + 1]))
+    for copy in copies:
+        copy.start()
+    for copy in copies:
+        copy.wait()
 
 
 def per_device(vis, station_pair_index, station_coords, dir_lm, time_beam, dir_cluster, seed_block):
@@ -422,16 +437,19 @@
     dpad = (dirs + 15) // 16 * 16
     stations = station_coords.shape[0]
     vmem = pl.BlockSpec(memory_space=pltpu.VMEM)
-    basis, gains, consensus = pl.pallas_call(
+    anywhere = pl.BlockSpec(memory_space=pl.ANY)
+    shapes = (
+        jax.ShapeDtypeStruct(vis.shape, BF16),
+        jax.ShapeDtypeStruct((tiles, CL), F32),
+        jax.ShapeDtypeStruct((1, CL), F32),
+    )
+    results = pl.pallas_call(
         functools.partial(main_kernel, n_chan, n_bl, chan_dev * n_chan),
-        out_shape=(
-            jax.ShapeDtypeStruct((tiles * rank, times), F32),
-            jax.ShapeDtypeStruct((tiles, CL), F32),
-            jax.ShapeDtypeStruct((1, CL), F32),
-        ),
-        in_specs=[pl.BlockSpec(memory_space=pl.ANY)] * 7,
-        out_specs=(vmem,) * 3,
+        out_shape=shapes,
+        in_specs=[anywhere] * 7,
+        out_specs=(anywhere, vmem, vmem),
         scratch_shapes=[
+            pltpu.VMEM(vis.shape, BF16),
             pltpu.VMEM(vis.shape, BF16),
             pltpu.VMEM((2, base_dev), jnp.int32),
             pltpu.VMEM((2, stations), F32),
@@ -455,6 +473,7 @@
             pltpu.SemaphoreType.DMA((SUB_ITERS + 3,)),
             pltpu.SemaphoreType.DMA((tiles,)),
             pltpu.SemaphoreType.DMA((6,)),
+            pltpu.SemaphoreType.DMA((tiles,)),
         ],
         compiler_params=pltpu.CompilerParams(
             collective_id=0, has_side_effects=True, vmem_limit_bytes=60 * 1024 * 1024
@@ -468,21 +487,14 @@
         dir_cluster.reshape(1, dirs),
         jnp.swapaxes(seed_block, 1, 2),
     )
-    spec = pl.BlockSpec((2, chan_dev, tile, times), lambda j: (0, 0, j, 0))
-    gains_spec = pl.BlockSpec((tiles, CL), lambda j: (0, 0))
-    cons_spec = pl.BlockSpec((1, CL), lambda j: (0, 0))
     clean, gains, consensus = pl.pallas_call(
-        clean_kernel,
-        grid=(tiles,),
-        out_shape=(
-            jax.ShapeDtypeStruct(vis.shape, BF16),
-            jax.ShapeDtypeStruct((tiles, CL), F32),
-            jax.ShapeDtypeStruct((1, CL), F32),
-        ),
-        in_specs=[spec, pl.BlockSpec((rank, times), lambda j: (j, 0)), gains_spec, cons_spec],
-        out_specs=(spec, gains_spec, cons_spec),
+        copy_kernel,
+        out_shape=shapes,
+        in_specs=[anywhere] * 3,
+        out_specs=(anywhere,) * 3,
+        scratch_shapes=[pltpu.SemaphoreType.DMA((2 * chan_dev + 2,))],
         compiler_params=pltpu.CompilerParams(vmem_limit_bytes=60 * 1024 * 1024),
-    )(vis, basis, gains, consensus)
+    )(*results)
     return clean, gains, consensus.reshape(CL)
 
 

time: 31.5 us -> 90.9 us (2.89)
  Pallas kernels: 30.7 us -> 90.1 us
    pallas_call x1, Pallas kernels: 4.79 us -> 64.8 us  [per_device(): pl.pallas_call(copy_kernel, out_shape=shapes, in_specs=[anywhere] * 3, ou...]
where the time goes in v3:
time: 90.9 us; the launch traced here: 90.8 us
  Pallas kernels  90.1 us (99%)
    pallas_call x1, Pallas kernels, per_device(): pl.pallas_call(copy_kernel, out_shape=shapes, in_specs=[anywhere] * 3, ou...  64.8 us
    pallas_call x1, Pallas kernels, per_device(): pl.pallas_call(functools.partial(main_kernel, n_chan, n_bl, chan_dev * n_...  25.3 us

profile of v3, /device:TPU:0, one launch (start us, length us, event | category | flops | bytes accessed | tf_op | source)
XLA Modules:
  0.0 90.8 jit_solution(11672436354492834900)
XLA Ops:
  0.6 25.3 %shard_map.94 = (bf16[2,4,512,256]{3,2,1,0:T(8,128)(2,1)}, f32[4,12]{1,0:T(4,128)}, f32[1,12]{1,0:T(1,128)}) custom-call(bf16[2,4,512,256]{3,2,1,0:T(8,128)(2,1)} %vis_hbm.1, s32[2,512]{1,0:T(2,128)} %bitcast.7, f32[2,512]{1,0:T(2,128)} %bitcast.8, f32[2,60]{1,0:T(2,128)} %bitcast.9, f32[60,256]{1,0:T(8,128)} %tb_hbm.1, s32[1,60]{1,0:T(1,128)} %bitcast.10, ...), custom_call_target="tpu_custom_call" | custom-call | tf_op jit(solution)/shard_map/pallas_call | solution.py:446
  26.0 64.8 %shard_map.95 = (bf16[2,4,512,256]{3,2,1,0:T(8,128)(2,1)}, f32[4,12]{1,0:T(4,128)}, f32[1,12]{1,0:T(1,128)}) custom-call(bf16[2,4,512,256]{3,2,1,0:T(8,128)(2,1)} %get-tuple-element.9.clean_in, f32[4,12]{1,0:T(4,128)} %get-tuple-element.10.gains_in, f32[1,12]{1,0:T(1,128)} %get-tuple-element.11.cons_in), custom_call_target="tpu_custom_call" | custom-call | tf_op jit(solution)/shard_map/pallas_call | solution.py:490

commit v4 on v3

--- a/solution.py
+++ b/solution.py
@@ -412,19 +412,21 @@
     sent(vbuf, n_all, SUB_ITERS + 2)
 
 
-def copy_kernel(clean_in, gains_in, cons_in, clean_out, gains_out, cons_out, sems):
+def copy_kernel(clean_in, gains_in, cons_in, clean_out, gains_out, cons_out, held, in_sems, out_sems):
+    gains_out[...] = gains_in[...]
+    cons_out[...] = cons_in[...]
     parts, chans = clean_in.shape[:2]
-    copies = [
-        pltpu.make_async_copy(clean_in.at[p, c], clean_out.at[p, c], sems.at[p * chans + c])
-        for p in range(parts)
-        for c in range(chans)
-    ]
-    copies.append(pltpu.make_async_copy(gains_in, gains_out, sems.at[parts * chans]))
-    copies.append(pltpu.make_async_copy(cons_in, cons_out, sems.at[parts * chans + 1]))
-    for copy in copies:
-        copy.start()
-    for copy in copies:
-        copy.wait()
+    blocks = [(p, c) for p in range(parts) for c in range(chans)]
+    loads, stores = [], []
+    for i, (p, c) in enumerate(blocks):
+        loads.append(pltpu.make_async_copy(clean_in.at[p, c], held.at[p, c], in_sems.at[i]))
+        stores.append(pltpu.make_async_copy(held.at[p, c], clean_out.at[p, c], out_sems.at[i]))
+        loads[i].start()
+    for i in range(len(blocks)):
+        loads[i].wait()
+        stores[i].start()
+    for store in stores:
+        store.wait()
 
 
 def per_device(vis, station_pair_index, station_coords, dir_lm, time_beam, dir_cluster, seed_block):
@@ -490,9 +492,13 @@
     clean, gains, consensus = pl.pallas_call(
         copy_kernel,
         out_shape=shapes,
-        in_specs=[anywhere] * 3,
-        out_specs=(anywhere,) * 3,
-        scratch_shapes=[pltpu.SemaphoreType.DMA((2 * chan_dev + 2,))],
+        in_specs=[anywhere, vmem, vmem],
+        out_specs=(anywhere, vmem, vmem),
+        scratch_shapes=[
+            pltpu.VMEM(vis.shape, BF16),
+            pltpu.SemaphoreType.DMA((2 * chan_dev,)),
+            pltpu.SemaphoreType.DMA((2 * chan_dev,)),
+        ],
         compiler_params=pltpu.CompilerParams(vmem_limit_bytes=60 * 1024 * 1024),
     )(*results)
     return clean, gains, consensus.reshape(CL)

time: 90.9 us -> 29.8 us (0.33)
  Pallas kernels: 90.1 us -> 29 us
    pallas_call x1, Pallas kernels: 64.8 us -> 3.66 us  [per_device(): pl.pallas_call(copy_kernel, out_shape=shapes, in_specs=[anywhere, vmem, v...]
where the time goes in v4:
time: 29.8 us; the launch traced here: 29.6 us
  Pallas kernels  29 us (97%)
  between operations  0.64 us (2%)
    pallas_call x1, Pallas kernels, per_device(): pl.pallas_call(functools.partial(main_kernel, n_chan, n_bl, chan_dev * n_...  25.3 us
    pallas_call x1, Pallas kernels, per_device(): pl.pallas_call(copy_kernel, out_shape=shapes, in_specs=[anywhere, vmem, v...  3.66 us

profile of v4, /device:TPU:0, one launch (start us, length us, event | category | flops | bytes accessed | tf_op | source)
XLA Modules:
  0.0 29.6 jit_solution(991898147595445164)
XLA Ops:
  0.6 25.3 %shard_map.94 = (bf16[2,4,512,256]{3,2,1,0:T(8,128)(2,1)}, f32[4,12]{1,0:T(4,128)}, f32[1,12]{1,0:T(1,128)}) custom-call(bf16[2,4,512,256]{3,2,1,0:T(8,128)(2,1)} %vis_hbm.1, s32[2,512]{1,0:T(2,128)} %bitcast.7, f32[2,512]{1,0:T(2,128)} %bitcast.8, f32[2,60]{1,0:T(2,128)} %bitcast.9, f32[60,256]{1,0:T(8,128)} %tb_hbm.1, s32[1,60]{1,0:T(1,128)} %bitcast.10, ...), custom_call_target="tpu_custom_call" | custom-call | tf_op jit(solution)/shard_map/pallas_call | solution.py:448
  26.0 3.7 %shard_map.95 = (bf16[2,4,512,256]{3,2,1,0:T(8,128)(2,1)}, f32[4,12]{1,0:T(4,128)}, f32[1,12]{1,0:T(1,128)}) custom-call(bf16[2,4,512,256]{3,2,1,0:T(8,128)(2,1)} %get-tuple-element.9.clean_in, f32[4,12]{1,0:T(4,128)} %get-tuple-element.10.gains_in, f32[1,12]{1,0:T(1,128)} %get-tuple-element.11.cons_in), custom_call_target="tpu_custom_call" | custom-call | tf_op jit(solution)/shard_map/pallas_call | solution.py:492
